TPU v7x, 32 devices: a whole 2x2x4 slice. The times are simulated.
32 devices in a mesh: dp: 8 (over y, x, core), mp: 4 (over z).
Axes of the slice: x: 2, y: 2, z: 4, core: 2. Of those that a mesh axis runs over, the one named last changes fastest.
Arguments:
- tokens: bfloat16 [128, 542, 768], P(('dp', 'mp')), may hold values from -6 to 6
- cotangent: bfloat16 [128, 542, 768], P(('dp', 'mp')), may hold values from -6 to 6
- kept_index: int32 [128, 268], P(('dp', 'mp')), may hold values from 0 to 541, as said below
- attention_weights: float32 [768, 3072], P(None, ('dp', 'mp')), may hold values from -0.4082483 to 0.4082483
- attention_first: float32 [768, 3072], P(None, ('dp', 'mp')), may hold values from -224 to 224
- attention_second: float32 [768, 3072], P(None, ('dp', 'mp')), may hold values from 1372.16 to 5488.64
- attention_average: float32 [768, 3072], P(None, ('dp', 'mp')), may hold values from -0.4082483 to 0.4082483
- feedforward_weights: float32 [2, 768, 3072], P(None, 'dp', 'mp'), may hold values from -0.14433757 to 0.14433757
- feedforward_first: float32 [2, 768, 3072], P(None, 'dp', 'mp'), may hold values from -448 to 448
- feedforward_second: float32 [2, 768, 3072], P(None, 'dp', 'mp'), may hold values from 5488.64 to 21954.56
- feedforward_average: float32 [2, 768, 3072], P(None, 'dp', 'mp'), may hold values from -0.14433757 to 0.14433757
- vector_weights: float32 [13, 768], replicated, may hold values from -1.2 to 1.3
- vector_first: float32 [13, 768], replicated, may hold values from -1024 to 1024
- vector_second: float32 [13, 768], replicated, may hold values from 34304 to 137216
- vector_average: float32 [13, 768], replicated, may hold values from -1.2 to 1.3
Outputs:
- block_output: bfloat16 [128, 542, 768], P(('dp', 'mp'))
- input_gradient: float32 [128, 542, 768], P(('dp', 'mp'))
- attention_gradient: float32 [768, 3072], P(None, ('dp', 'mp'))
- attention_first_new: float32 [768, 3072], P(None, ('dp', 'mp'))
- attention_second_new: float32 [768, 3072], P(None, ('dp', 'mp'))
- attention_weights_new: float32 [768, 3072], P(None, ('dp', 'mp'))
- attention_average_new: float32 [768, 3072], P(None, ('dp', 'mp'))
- attention_copy: bfloat16 [768, 3072], P(None, ('dp', 'mp'))
- feedforward_gradient: float32 [2, 768, 3072], P(None, 'dp', 'mp')
- feedforward_first_new: float32 [2, 768, 3072], P(None, 'dp', 'mp')
- feedforward_second_new: float32 [2, 768, 3072], P(None, 'dp', 'mp')
- feedforward_weights_new: float32 [2, 768, 3072], P(None, 'dp', 'mp')
- feedforward_average_new: float32 [2, 768, 3072], P(None, 'dp', 'mp')
- feedforward_copy: bfloat16 [2, 768, 3072], P(None, 'dp', 'mp')
- vector_gradient: float32 [13, 768], replicated
- vector_first_new: float32 [13, 768], replicated
- vector_second_new: float32 [13, 768], replicated
- vector_weights_new: float32 [13, 768], replicated
- vector_average_new: float32 [13, 768], replicated
- query_bias_gradient: float32 [768], replicated
Inputs may be any that keep to these rules, and one draw needn't show every extreme that they name: `kept_index`: for each image and each of its six crops in order, 197//2 (global crops) or 37//2 (local crops) distinct increasing positions inside that crop; the crop's first and last positions are always among them.
All inputs are finite; a program needn't handle non-finite values.
Results may differ from a plain program's by a relative error of at most 0.0098.
The roundings to bfloat16 on the way count: a program that leaves them out, or rounds other values in their place, can miss the bound.
Values may be sent and summed in bfloat16 or wider, within the bound.
A program may use at most 192 MiB of HBM per device.

v0:
```python
import functools

import jax
import jax.numpy as jnp
import numpy as np
from jax import lax
from jax.experimental import pallas as pl
from jax.experimental.pallas import tpu as pltpu
from jax.sharding import PartitionSpec as P

H = 12
HD = 64
LG = 197
LL = 37
KG = LG // 2
KL = LL // 2
LOC = 4 * KL
KEPT = 2 * KG + LOC
RI = -(-KEPT // 16) * 16
SPANS = ((0, KG), (KG, 2 * KG), (2 * KG, KEPT))
UNITS = tuple((a // 16 * 16, -(-b // 16) * 16) for a, b in SPANS)
PAIRS = H // 2
W2L = 2 * HD

bf16 = jnp.bfloat16
f32 = jnp.float32


def params(limit=56, **kw):
    return pltpu.CompilerParams(vmem_limit_bytes=limit << 20, **kw)


def full(shape):
    return pl.BlockSpec(shape, lambda *_: (0,) * len(shape))


def per_image(*shape):
    return pl.BlockSpec((1,) + shape, lambda i, *_: (i,) + (0,) * len(shape))


def nn(a, b):
    return lax.dot_general(a, b, (((1,), (0,)), ((), ())), preferred_element_type=f32)


def nt(a, b):
    return lax.dot_general(a, b, (((1,), (1,)), ((), ())), preferred_element_type=f32)


def tn(a, b):
    return lax.dot_general(a, b, (((0,), (0,)), ((), ())), preferred_element_type=f32)


def normalize(rows):
    center = rows - jnp.mean(rows, axis=-1, keepdims=True)
    spread = jnp.mean(center * center, axis=-1, keepdims=True)
    inverse = lax.rsqrt(spread + 1e-06)
    return center * inverse, inverse


def norm_backward(upstream, standard, inverse, gain):
    scaled = upstream * gain
    return inverse * (
        scaled
        - jnp.mean(scaled, axis=-1, keepdims=True)
        - standard * jnp.mean(scaled * standard, axis=-1, keepdims=True)
    )


def colsum(v):
    return jnp.sum(v, axis=0, keepdims=True)


def masks():
    crop = np.full(RI, -1)
    crop[:KG], crop[KG : 2 * KG] = 0, 1
    for c in range(4):
        crop[2 * KG + c * KL : 2 * KG + (c + 1) * KL] = 2 + c
    adds, valids = [], []
    for (a, b), (lo, hi) in zip(SPANS, UNITS):
        rows = np.arange(lo, hi)
        inside = (rows >= a) & (rows < b)
        same = (crop[lo:hi, None] == crop[None, lo:hi]) & inside[:, None] & inside[None, :]
        adds.append(np.tile(np.where(same, 0.0, -1e9), (1, 2)).astype(np.float32))
        valids.append(np.tile(inside[None, :].astype(np.float32), (8, 2)))
    return [jnp.asarray(m) for m in adds + valids]


def lane_half(shape):
    return lax.broadcasted_iota(jnp.int32, shape, len(shape) - 1) < HD


def split_heads(v, scale):
    first = lane_half(v.shape)
    zero = jnp.zeros_like(v)
    if scale != 1.0:
        v = v * jnp.asarray(scale, v.dtype)
    return jnp.concatenate([jnp.where(first, v, zero), jnp.where(first, zero, v)], axis=0)


def join_heads(v):
    n = v.shape[0] // 2
    return jnp.where(lane_half((n, v.shape[1])), v[:n], v[n:])


def softmax_keys(st, valid):
    p = jnp.exp(st - jnp.max(st, axis=0, keepdims=True))
    return p * (valid / jnp.sum(p, axis=0, keepdims=True))


def store_window(ref, image, lo, hi, last, cols, value, tail):
    value = value.astype(bf16)
    if tail is not None:
        value = jnp.concatenate([value[:16] + tail, value[16:]], axis=0)
    end = hi if last else hi - 16
    ref[image, lo:end, cols] = value[: end - lo]
    return None if last else value[end - lo :]


MESH = pl.DeviceIdType.MESH
ANY = pl.BlockSpec(memory_space=pl.ANY)
MP = 4
CROPS = ((0, LG), (LG, 2 * LG), (2 * LG, 2 * LG + 4 * LL))
ORDER = ((0, 1, 2, 3), (1, 0, 1, 2), (2, 2, 3, 1), (3, 3, 0, 0))


def flip(index, bit):
    return index + bit * (1 - 2 * lax.rem(lax.div(index, bit), 2))


def remote(src, dst, send, recv, to):
    return pltpu.make_async_remote_copy(
        src_ref=src, dst_ref=dst, send_sem=send, recv_sem=recv, device_id=to, device_id_type=MESH
    )


class Sends:
    def __init__(self):
        self.made = []

    def start(self, make, when=None):
        def go():
            make().start()

        go() if when is None else pl.when(when)(go)
        self.made.append((make, when))

    def finish(self):
        for make, when in self.made:
            def wait(make=make):
                make().wait_send()

            wait() if when is None else pl.when(when)(wait)


class Place:
    def __init__(self):
        self.dp = lax.axis_index("dp")
        self.z = lax.axis_index("mp")
        x, y = flip(self.dp, 2), flip(self.dp, 4)
        self.core = (flip(self.dp, 1), self.z)
        self.x, self.y = (x, self.z), (y, self.z)
        self.chips = (self.dp, x, y, flip(x, 4))
        self.mates = tuple(flip(c, 1) for c in self.chips)
        power = (1 + 3 * lax.rem(self.z, 2)) * (1 + 15 * lax.div(self.z, 2))
        self.event = []
        for row in ORDER:
            code = sum(v << (2 * i) for i, v in enumerate(row))
            self.event.append(lax.rem(lax.div(0 * power + code, power), 4))
        self.low, self.high = self.z > 0, self.z < MP - 1
        self.middle = self.low & self.high
        self.line = [lax.rem(self.z + k, MP) for k in range(MP)]
        self.up, self.down = (self.dp, self.z + 1), (self.dp, self.z - 1)
        self.onward = (self.up, self.down, (self.dp, 3 * (self.z - 1)))

    def barrier(self):
        sem = pltpu.get_barrier_semaphore()
        others = [self.core, self.x, self.y]
        others += [(self.dp, k) for k in self.line[1:]]
        for other in others:
            pl.semaphore_signal(sem, inc=1, device_id=other, device_id_type=MESH)
        pl.semaphore_wait(sem, len(others))


def att_block(ref, dp, z, rows):
    return ref.at[pl.ds(pl.multiple_of((dp * MP + z) * rows, 32), rows), :]


def att_part(ref, dp, z, rows, h):
    half = rows // 2
    return ref.at[pl.ds(pl.multiple_of((dp * MP + z) * rows + h * half, 16), half), :]


def ff_part(ref, dp, z, rows, h):
    return ref.at[z, h, pl.ds(pl.multiple_of(dp * rows, 32), rows), :]


def ff_block(ref, dp, z, rows):
    return ref.at[z, :, pl.ds(pl.multiple_of(dp * rows, 32), rows), :]


class Gather:
    ALONG, X, Y, D, C, SLOTS = 0, 4, 8, 12, 16, 32

    def __init__(self, at, first, place, send, recv, local):
        self.at, self.first, self.place = at, first, place
        self.send, self.recv, self.local = send, recv, local
        self.sends = Sends()

    def copy(self, slot, e, r, to):
        slot = self.ALONG + self.at.event[e] if slot is None else slot
        dst = self.place(e, self.at.chips[r])
        src = self.first(e) if r == 0 else dst
        return remote(src, dst, self.send.at[slot], self.recv.at[slot], to)

    def put(self, slot, e, r, to, when=None):
        self.sends.start(lambda: self.copy(slot, e, r, to), when)

    def got(self, slot, e, dp):
        dst = self.place(e, dp)
        remote(dst, dst, self.send.at[slot], self.recv.at[slot], self.at.core).wait_recv()

    def keep(self, e):
        return pltpu.make_async_copy(self.first(e), self.place(e, self.at.dp), self.local.at[e])

    def spread(self, e):
        self.put(self.X + e, e, 0, self.at.x)
        self.put(self.Y + e, e, 0, self.at.y)
        self.put(self.C + 4 * e, e, 0, self.at.core)

    def begin(self):
        at = self.at
        self.keep(0).start()
        for to, when in ((at.up, at.high), (at.down, at.low)):
            self.put(None, 0, 0, to, when)
        self.spread(0)

    def direct(self):
        self.keep(0).start()
        for zb in self.at.line[1:]:
            self.put(None, 0, 0, (self.at.dp, zb))

    def arrived(self, e):
        self.got(self.ALONG + self.at.event[e], e, self.at.dp)

    def along(self, e):
        at = self.at
        self.arrived(e)
        self.put(None, e, 0, at.onward[e - 1], at.middle)
        self.spread(e)

    def plane(self, e):
        at = self.at
        self.got(self.X + e, e, at.chips[1])
        if e % 2 == 0:
            self.put(self.D + e, e, 1, at.y)
        self.put(self.C + 4 * e + 1, e, 1, at.core)
        self.got(self.Y + e, e, at.chips[2])
        if e % 2 == 1:
            self.put(self.D + e, e, 2, at.x)
        self.put(self.C + 4 * e + 2, e, 2, at.core)

    def corner(self, e):
        self.got(self.D + e, e, self.at.chips[3])
        self.put(self.C + 4 * e + 3, e, 3, self.at.core)

    def finish(self, e):
        for r in range(4):
            self.got(self.C + 4 * e + r, e, self.at.mates[r])


def add_into(target, first, *others):
    if len(others) == 1 and target.dtype == bf16:
        @pl.loop(0, first.shape[0] // 48)
        def _(i):
            s = pl.ds(pl.multiple_of(i * 48, 16), 48)
            target[s, :] = first[s, :] + others[0][s, :]

        return
    step = 48

    @pl.loop(0, first.shape[0] // step)
    def _(i):
        s = pl.ds(pl.multiple_of(i * step, 16), step)
        total = first[s, :].astype(f32)
        for ref in others:
            total = total + ref[s, :].astype(f32)
        target[s, :] = total.astype(target.dtype)


class Reduce:
    C, D, X, Y, ALONG, SLOTS = 0, 16, 20, 24, 28, 32

    def __init__(self, at, source, own, parts, bufs, send, recv, load=None, base=0):
        self.at, self.source, self.own, self.parts, self.base = at, source, own, parts, base
        self.c, self.d, self.x, self.y, self.line = bufs
        self.send, self.recv, self.load = send, recv, load
        self.sends = Sends()

    def put(self, slot, src, dst, to):
        self.sends.start(
            lambda: remote(src(), dst(), self.send.at[slot], self.recv.at[slot], to)
        )

    def got(self, slot, dst):
        remote(dst, dst, self.send.at[slot], self.recv.at[slot], self.at.core).wait_recv()

    def slot(self, e, r):
        return 4 * (e - self.base) + r

    def cross(self, e, r):
        i = self.slot(e, r)
        self.put(self.C + i, lambda: self.source(e, self.at.mates[r]), lambda: self.c.at[i], self.at.core)
        if self.load is not None:
            self.load(e, r).start()

    def add(self, e, r, *others, target=None):
        i = self.slot(e, r)
        self.got(self.C + i, self.c.at[i])
        if self.load is not None:
            self.load(e, r).wait()
        refs = [self.own(e, r), self.c.at[i]] + list(others)
        self.total(refs[0] if target is None else target, *refs)

    def total(self, target, *refs):
        for t, *rest in zip(self.parts(target), *[self.parts(ref) for ref in refs]):
            add_into(t, *rest)

    def corner(self, e):
        at, i = self.at, e - self.base
        self.add(e, 3)
        self.put(
            self.D + i, lambda: self.own(e, 3), lambda: self.d.at[i], at.x if e % 2 else at.y
        )
        r, slot, buf, to = (1, self.X, self.x, at.x) if e % 2 else (2, self.Y, self.y, at.y)
        self.add(e, r)
        self.put(slot + i, lambda: self.own(e, r), lambda: buf.at[i], to)

    def plane(self, e):
        at, i = self.at, e - self.base
        r, slot, buf, to = (2, self.Y, self.y, at.y) if e % 2 else (1, self.X, self.x, at.x)
        self.got(self.D + i, self.d.at[i])
        self.add(e, r, self.d.at[i])
        self.put(slot + i, lambda: self.own(e, r), lambda: buf.at[i], to)

    def gathered(self, e, *others, target=None):
        i = e - self.base
        self.got(self.X + i, self.x.at[i])
        self.got(self.Y + i, self.y.at[i])
        self.add(e, 0, self.x.at[i], self.y.at[i], *others, target=target)

    def send_along(self, e, src):
        at = self.at
        zb = at.event[e]
        self.sends.start(
            lambda: remote(
                src(), self.line.at[at.z], self.send.at[self.ALONG + zb],
                self.recv.at[self.ALONG + at.z], (at.dp, zb),
            )
        )

    def along(self, e):
        self.gathered(e)
        self.send_along(e, lambda: self.own(e, 0))

    def lines(self):
        got = []
        for zb in self.at.line[1:]:
            got.append(self.line.at[zb])
            self.got(self.ALONG + zb, got[-1])
        return got


def pump(schedule, step, point):
    for (s, p), action in schedule:
        if isinstance(point, int):
            if p == point:
                pl.when(step == s)(action)
        else:
            pl.when((step == s) & (point == p))(action)


def do(action, *args):
    return lambda: action(*args)


def token_columns(idx_ref, idx_s, col_s):
    idx_s[...] = jnp.full(idx_s.shape, -1.0, f32)
    idx_s[0 : idx_ref.shape[0], 0 : idx_ref.shape[1]] = idx_ref[...].astype(f32)
    col_s[...] = idx_s[...].T


def one_hot(col_s, crop, images, local):
    (a, b), (s, e), (lo, hi) = [v[2 if local else 0] for v in (CROPS, SPANS, UNITS)]
    n, size = hi - lo, b - a
    count = images * size
    if not local:
        a, s, e, lo = LG * crop, KG * crop, KG * (crop + 1), UNITS[1][0] * crop
        lo = pl.multiple_of(lo, 16)
    columns = col_s[pl.ds(lo, n), :]
    row = lax.broadcasted_iota(jnp.int32, (n, 1), 0) + lo
    pieces = []
    for i in range(images):
        place = (columns[:, i : i + 1].astype(jnp.int32) - a) * images + i
        pieces.append(jnp.where((row >= s) & (row < e), place, -1))
    index = jnp.concatenate(pieces, axis=0)
    hot = lax.broadcasted_iota(jnp.int32, (index.shape[0], count), 1) == index
    return hot.astype(f32).astype(bf16), pl.ds(a, size), lo, n, count


def forward_kernel(
    links, tok_ref, cot_ref, idx_ref, vec_ref, m0_ref, m1_ref, m2_ref, v0_ref, v1_ref, v2_ref,
    att_ref, ff_ref,
    kept_ref, normed_ref, cotk_ref, proj_ref, mixed_ref, branch_ref, resid_ref, n2_ref,
    watt_out, *rest,
):
    if links:
        wff_ref, watt_ref, tok_s, cot_s, idx_s, col_s, load, att_s, ff_s, send, recv, local = rest
    else:
        watt_ref, tok_s, cot_s, idx_s, col_s, load = rest
    step = pl.program_id(0)
    images, _, d = kept_ref.shape
    loads = [
        pltpu.make_async_copy(tok_ref, tok_s, load.at[0]),
        pltpu.make_async_copy(cot_ref, cot_s, load.at[1]),
    ]
    acts, schedule = [[]] * 6, []
    if links:
        at = Place()
        rows = att_ref.shape[0]
        half = rows // 2

        def att_half(h):
            return Gather(
                at,
                lambda e: att_part(watt_ref, at.dp, at.event[e], rows, h) if e
                else att_s.at[h * half : (h + 1) * half],
                lambda e, dp: att_part(watt_ref, dp, at.event[e], rows, h),
                send.at[h], recv.at[h], local.at[h],
            )

        def feed_half(h):
            return Gather(
                at, lambda e: ff_part(wff_ref, at.dp, at.event[e], rows, h) if e else ff_s.at[h],
                lambda e, dp: ff_part(wff_ref, dp, at.event[e], rows, h),
                send.at[2 + h], recv.at[2 + h], local.at[2 + h],
            )

        (a0, a1), (f0, f1) = [att_half(h) for h in (0, 1)], [feed_half(h) for h in (0, 1)]
        acts = [
            [a1.begin, a0.begin],
            [do(a1.along, 1), do(a1.plane, 0), do(a0.along, 1), do(a0.along, 2), do(a1.along, 2)],
            [do(a0.along, 3)],
            [do(a1.along, 3), f0.direct, do(a1.plane, 1), do(a0.plane, 2)],
            [do(a0.plane, 0)],
            [
                do(a0.plane, 3), do(a0.plane, 1), do(a1.plane, 3), do(a1.plane, 2),
                do(a0.corner, 0), do(a1.corner, 1), do(a0.corner, 3), do(a1.corner, 2),
                do(a1.corner, 0), f1.direct, do(a0.corner, 1), do(a0.corner, 2), do(a1.corner, 3),
                do(f0.arrived, 2), do(f0.spread, 2),
            ],
        ]
        schedule = [
            ((1, 3), do(f0.arrived, 3)),
            ((1, 3), do(f0.spread, 3)),
            ((2, 1), do(f1.arrived, 2)),
            ((2, 1), do(f1.spread, 2)),
            ((3, 0), do(f1.arrived, 3)),
            ((3, 0), do(f1.spread, 3)),
            ((3, 0), do(f0.plane, 2)),
            ((3, 1), do(f1.plane, 2)),
            ((3, 1), do(f0.plane, 3)),
            ((3, 3), do(f1.plane, 3)),
            ((4, 3), do(f1.corner, 3)),
            ((4, 3), do(f0.corner, 3)),
            ((4, 3), do(f1.corner, 2)),
            ((4, 3), do(f0.corner, 2)),
        ]
    else:
        fetch = pltpu.make_async_copy(att_ref, watt_ref, load.at[2])
    store = pltpu.make_async_copy(watt_ref, watt_out, load.at[2])

    def clear(dst):
        for i in range(images):
            for _, hi in UNITS[:2]:
                dst[i, hi - 16 : hi] = jnp.zeros((16, d), bf16)

    def pick(crop, local, src, dst):
        hot, span, lo, n, k = one_hot(col_s, crop, images, local)
        got = nn(hot, src[span].reshape(k, d)).astype(bf16)
        for i in range(images):
            part = got[i * n : (i + 1) * n]
            head = pl.ds(lo, 16)
            if local:
                dst[i, head, :] = dst[i, head, :] + part[:16]
            else:
                old = jnp.where(crop == 0, jnp.zeros_like(part[:16]), dst[i, head, :])
                dst[i, head, :] = old + part[:16]
            dst[i, pl.ds(lo + 16, n - 16), :] = part[16:]

    def run(point):
        for action in acts[point]:
            action()

    @pl.when(step == 0)
    def _():
        if links:
            att_s[...] = att_ref[...].astype(bf16)
            at.barrier()
            run(0)
        else:
            fetch.start()
        for c in loads:
            c.start()
        if links:
            ff_s[...] = ff_ref[...].astype(bf16)
        token_columns(idx_ref, idx_s, col_s)
        loads[0].wait()
        clear(kept_ref)

        @pl.loop(0, 2)
        def _(crop):
            pick(crop, False, tok_s, kept_ref)
            for point in (1, 2):
                pl.when(crop == point - 1)(do(run, point))

        pick(2, True, tok_s, kept_ref)
        run(3)
        for i in range(images):
            standard, _ = normalize(kept_ref[i].astype(f32))
            normed_ref[i] = (standard * vec_ref[0:1] + vec_ref[1:2]).astype(bf16)
            if i == 1:
                run(4)
        run(5)
        if links:
            for e in range(4):
                a0.finish(e)
                a1.finish(e)
            a0.keep(0).wait()
            a1.keep(0).wait()
        else:
            fetch.wait()
        store.start()

    pump(schedule, step, 0)

    @pl.when(step > 0)
    def _():
        image = step - 1
        normed = normed_ref[image]
        for j, row in ((0, 3), (1, None), (2, 4)):
            part = nt(normed, watt_ref[j * d : (j + 1) * d, :])
            if row is not None:
                part = part + vec_ref[row : row + 1]
            proj_ref[0, :, j * d : (j + 1) * d] = part.astype(bf16)
        pump(schedule, step, 1)

        @pl.when(step == 2)
        def _():
            loads[1].wait()
            clear(cotk_ref)

        @pl.when((step == 2) | (step == 3))
        def _():
            pick(step - 2, False, cot_s, cotk_ref)

        @pl.when(step == 4)
        def _():
            pick(2, True, cot_s, cotk_ref)

        mrefs, vrefs = (m0_ref, m1_ref, m2_ref), (v0_ref, v1_ref, v2_ref)
        for pair in range(PAIRS):
            cols = lambda j: slice(j * d + pair * W2L, j * d + (pair + 1) * W2L)
            tail = None
            for unit, (lo, hi) in enumerate(UNITS):
                qs = split_heads(proj_ref[0, lo:hi, cols(0)], HD ** -0.5)
                st = nt(proj_ref[0, lo:hi, cols(1)], qs) + mrefs[unit][...]
                pt = softmax_keys(st, vrefs[unit][0:1]).astype(bf16)
                out = join_heads(tn(pt, proj_ref[0, lo:hi, cols(2)]))
                tail = store_window(mixed_ref, 0, lo, hi, unit == 2, cols(0), out, tail)
            if pair == 2:
                pump(schedule, step, 3)
        branch = nt(mixed_ref[0], watt_ref[3 * d :, :]) + vec_ref[5:6]
        branch_ref[0] = branch
        residual = kept_ref[image].astype(f32) + router_score(normed, vec_ref) * branch
        resid_ref[0] = residual
        standard, _ = normalize(residual)
        n2_ref[0] = (standard * vec_ref[6:7] + vec_ref[7:8]).astype(bf16)

    @pl.when(step == images)
    def _():
        if links:
            for feed in (f0, f1):
                feed.finish(2)
                feed.finish(3)
                feed.arrived(1)
                feed.keep(0).wait()
            for part in (a0, a1, f0, f1):
                part.sends.finish()
        store.wait()


def router_score(normed, vec_ref):
    logit = jnp.sum(normed.astype(f32) * vec_ref[2:3], axis=-1, keepdims=True)
    return jax.nn.sigmoid(logit)


def feed_kernel(
    links, n2_ref, cot_ref, resid_ref, w_ref, vec_ref,
    result_ref, n2g_ref, gff_ref, bg_ref, *rest,
):
    if links:
        acc_ref, out_s, act_s, ig_s, i0, i1, a0, a1, w_s, g_s, load, store = rest[:12]
        send, recv, local, a, c, dd, x, y, rsend, rrecv, rlocal = rest[12:]
    else:
        out_s, act_s, ig_s, i0, i1, a0, a1, w_s, g_s, load, store = rest
    inner_s, ag_s = (i0, i1), (a0, a1)
    step = pl.program_id(0)
    last = pl.num_programs(0) - 1
    images, _, d = n2_ref.shape
    nload = w_s.shape[0]
    hb = w_ref.shape[3]
    block, schedule = step, []
    if links:
        at = Place()
        rows = acc_ref.shape[2]
        block = at.event[0]
        for e in (1, 2, 3):
            block = jnp.where(step == 3 - e, at.event[e], block)
        gather = Gather(
            at, lambda e: ff_block(w_ref, at.dp, at.event[e], rows),
            lambda e, dp: w_s.at[3 - e, :, pl.ds(pl.multiple_of(dp * rows, 32), rows), :],
            send, recv, local,
        )
        reduce = Reduce(
            at, lambda e, dp: ff_block(gff_ref, dp, at.event[e], rows),
            lambda e, r: a.at[4 * (e - 2) + r],
            lambda ref: (ref.at[0], ref.at[1]), (c, dd, x, y, None), rsend, rrecv,
            lambda e, r: pltpu.make_async_copy(
                ff_block(gff_ref, at.chips[r], at.event[e], rows), a.at[4 * (e - 2) + r],
                rlocal.at[4 * (e - 2) + r],
            ),
            2,
        )

        def start():
            at.barrier()
            for e in (1, 0):
                gather.spread(e)
                gather.keep(e).start()

        def ready(e):
            gather.finish(e)
            gather.keep(e).wait()

        def cross(e):
            for r in (3, 1, 2, 0):
                reduce.cross(e, r)

        schedule = [
            ((1, 0), do(gather.plane, 1)),
            ((1, 3), do(gather.plane, 0)),
            ((1, 4), do(cross, 3)),
            ((2, 0), do(gather.corner, 1)),
            ((2, 0), do(reduce.corner, 3)),
            ((2, 0), do(cross, 2)),
            ((2, 0), do(ready, 1)),
            ((2, 2), do(reduce.corner, 2)),
            ((2, 2), do(gather.corner, 0)),
            ((2, 5), do(reduce.plane, 3)),
            ((3, 0), do(ready, 0)),
            ((3, 0), do(reduce.plane, 2)),
        ]

    def fetch(e):
        return pltpu.make_async_copy(
            w_ref.at[at.event[3 - e] if links else e], w_s.at[e], load.at[e]
        )

    def save(slot, which):
        return pltpu.make_async_copy(g_s.at[slot], gff_ref.at[which], store.at[slot])

    residual = pltpu.make_async_copy(resid_ref, out_s, load.at[nload])
    early = (0, 1) if links else range(w_s.shape[0])

    @pl.when(step == 0)
    def _():
        for e in early:
            fetch(e).start()
        if links:
            start()
        residual.start()
        n2g_ref[...] = jnp.zeros_like(n2g_ref)
        bg_ref[...] = jnp.zeros_like(bg_ref)
        fetch(0).wait()
        residual.wait()

    for e in early[1:]:
        @pl.when(step == e)
        def _(e=e):
            fetch(e).wait()

    slot = lax.rem(step, 2)

    @pl.when(step > 0)
    def _():
        save(1 - slot, 0).wait()

    pump(schedule, step, 0)

    def first(i):
        inner_s[i % 2][...] = nn(n2_ref[i], w_s[step, 0]) + vec_ref[pl.ds(9 + block, 1), :]
        ag_s[i % 2][...] = nn(cot_ref[i], w_s[step, 1])

    def second(i):
        inner = inner_s[i % 2][...]
        phi = 0.5 * (1.0 + lax.erf(inner * 0.7071067811865476))
        act = (inner * phi).astype(bf16)
        slope = phi + inner * jnp.exp(-0.5 * inner * inner) * 0.3989422804014327
        ig = (ag_s[i % 2][...] * slope).astype(bf16)
        rows_i = slice(i * RI, (i + 1) * RI)
        act_s[rows_i, :] = act
        ig_s[rows_i, :] = ig
        bg_ref[pl.ds(block, 1), :] += colsum(ig.astype(f32))
        out_s[i] += nt(act, w_s[step, 1])
        n2g_ref[i] += nt(ig, w_s[step, 0])

    first(0)
    for i in range(images):
        pump(schedule, step, i + 1)
        if i + 1 < images:
            first(i + 1)
        second(i)

    pump(schedule, step, 5)
    n2 = n2_ref[...].reshape(images * RI, d)
    cot = cot_ref[...].reshape(images * RI, d)
    g_s[slot, 0] = tn(n2, ig_s[...]).astype(bf16)
    g_s[slot, 1] = tn(cot, act_s[...]).astype(bf16)
    save(slot, block).start()

    @pl.when(step == last)
    def _():
        result_ref[...] = (out_s[...] + vec_ref[8:9]).astype(bf16)
        if links:
            reduce.gathered(3, target=acc_ref.at[0])
            reduce.gathered(2, target=acc_ref.at[1])
            gather.sends.finish()
            reduce.sends.finish()
        save(slot, 0).wait()


def backward_kernel(
    links, n2g_ref, cotk_ref, branch_ref, resid_ref, normed_ref, proj_ref, wout_ref,
    vec_ref, m0_ref, m1_ref, m2_ref, v0_ref, v1_ref, v2_ref, *rest,
):
    if links:
        gff_ref, acc_ref, dp_ref, resg_ref, rg_ref, vecg_ref, gout_ref = rest[:7]
        mg_s, a, c, dd, x, y, line, send, recv, local = rest[7:]
    else:
        dp_ref, resg_ref, rg_ref, vecg_ref, mg_s = rest
    step = pl.program_id(0)
    schedule = []
    if links:
        at = Place()
        rows = gout_ref.shape[1]
        reduce = Reduce(
            at, lambda e, dp: ff_block(gff_ref, dp, at.event[e], rows),
            lambda e, r: a.at[4 * e + r],
            lambda ref: (ref.at[0], ref.at[1]), (c, dd, x, y, line), send, recv,
            lambda e, r: pltpu.make_async_copy(
                ff_block(gff_ref, at.chips[r], at.event[e], rows), a.at[4 * e + r],
                local.at[4 * e + r],
            ),
        )

        def start():
            at.barrier()
            reduce.send_along(2, lambda: acc_ref.at[1])
            for e in (1, 0):
                for r in (3, 1, 2, 0):
                    reduce.cross(e, r)

        schedule = [
            ((0, 0), start),
            ((0, 1), do(reduce.corner, 1)),
            ((0, 3), do(reduce.send_along, 3, lambda: acc_ref.at[0])),
            ((1, 1), do(reduce.plane, 1)),
            ((1, 3), do(reduce.corner, 0)),
            ((2, 1), do(reduce.along, 1)),
            ((3, 0), do(reduce.plane, 0)),
        ]

    pump(schedule, step, 0)
    d = normed_ref.shape[2]
    normed = normed_ref[0]
    score = router_score(normed, vec_ref)
    branch = branch_ref[0]
    standard, inverse = normalize(resid_ref[0])
    n2g = n2g_ref[0]
    cot = cotk_ref[0].astype(f32)
    resg = cot + norm_backward(n2g, standard, inverse, vec_ref[6:7])
    resg_ref[0] = resg
    bg = (score * resg).astype(bf16)
    rg = jnp.sum(resg * branch, axis=-1, keepdims=True) * score * (1.0 - score)
    rg_ref[0] = rg
    dp_ref[0, :, 3 * d :] = bg
    mg_s[...] = nn(bg, wout_ref[...]).astype(bf16)
    pump(schedule, step, 1)
    mrefs, vrefs = (m0_ref, m1_ref, m2_ref), (v0_ref, v1_ref, v2_ref)
    for pair in range(PAIRS):
        cols = lambda j: slice(j * d + pair * W2L, j * d + (pair + 1) * W2L)
        tails = [None] * 3
        for unit, (lo, hi) in enumerate(UNITS):
            qs = split_heads(proj_ref[0, lo:hi, cols(0)], HD ** -0.5)
            kk = proj_ref[0, lo:hi, cols(1)]
            pt = softmax_keys(nt(kk, qs) + mrefs[unit][...], vrefs[unit][0:1])
            ds = split_heads(mg_s[lo:hi, cols(0)], 1.0)
            gpt = nt(proj_ref[0, lo:hi, cols(2)], ds)
            sg = (pt * (gpt - jnp.sum(pt * gpt, axis=0, keepdims=True))).astype(bf16)
            grads = (
                join_heads(tn(sg, kk)) * HD ** -0.5, nn(sg, qs), nn(pt.astype(bf16), ds)
            )
            for j in range(3):
                tails[j] = store_window(dp_ref, 0, lo, hi, unit == 2, cols(j), grads[j], tails[j])
        if pair == 2:
            pump(schedule, step, 3)
    sums = jnp.concatenate(
        [
            colsum(rg * normed.astype(f32)),
            colsum(dp_ref[0, :, :d].astype(f32)),
            colsum(dp_ref[0, :, 2 * d : 3 * d].astype(f32)),
            colsum(bg.astype(f32)),
            colsum(n2g * standard),
            colsum(n2g),
            colsum(cot),
            jnp.zeros((1, d), f32),
        ],
        axis=0,
    )

    @pl.when(step == 0)
    def _():
        vecg_ref[...] = jnp.zeros_like(vecg_ref)

    vecg_ref[...] += sums
    if links:
        @pl.when(step == pl.num_programs(0) - 1)
        def _():
            reduce.gathered(0, *reduce.lines(), target=gout_ref)
            reduce.sends.finish()


def grads_kernel(
    links, dp_ref, normed_ref, mixed_ref, rg_ref, resg_ref, kept_ref, vec_ref, watt_ref,
    idx_ref, tok_ref, cot_ref, result_ref, *rest,
):
    if links:
        vecb_ref, bias_ref, ing_ref, out_ref, gout_ref, vecout_ref = rest[:6]
        gatt_s, vecg_s, *rest = rest[6:]
        c, dd, x, y, line, send, recv, vbuf, vsend, vrecv = rest[17:]
    else:
        ing_ref, out_ref, gatt_s, vecg_s, *rest = rest
    watt_s, dp_s, act_s, resg_s, kept_s, load, high_ref, low_ref, result_s = rest[:9]
    idx_s, col_s, tok_s, cot_s, ing_s, out_s, fetch, store = rest[9:17]
    step = pl.program_id(0)
    images, _, d = high_ref.shape
    last = 3 + images + 3
    total = images * RI
    chip, schedule = 0, []
    if links:
        at = Place()
        chip = lax.div(at.dp, 2)
        rows = gout_ref.shape[0]
        block = lambda e, dp: att_block(gatt_s, dp, at.event[e], rows)
        reduce = Reduce(
            at, block, lambda e, r: block(e, at.chips[r]), lambda ref: (ref,),
            (c, dd, x, y, line), send, recv,
        )

        def cross(r):
            for e in (3, 2, 1, 0):
                reduce.cross(e, r)

        exchange = lambda k, to: remote(
            vbuf.at[k + 1], vbuf.at[8 + k], vsend.at[k], vrecv.at[k], to
        )
        lines = [
            lambda k=k: remote(
                vbuf.at[0], vbuf.at[4 + at.z], vsend.at[2 + k], vrecv.at[3 + at.z],
                (at.dp, at.line[k]),
            )
            for k in range(1, MP)
        ]

        def spread_vectors():
            vbuf[0, 0:2] = vecg_s[0:2]
            vbuf[0, 2:9] = vecb_ref[0:7]
            vbuf[0, 9:13] = bias_ref[...]
            vbuf[0, 13:16] = jnp.zeros((3, d), f32)
            for make in lines:
                make().start()
            vbuf[4 + at.z] = vbuf[0]

        def line_vectors():
            for k in range(1, MP):
                zb = at.line[k]
                remote(
                    vbuf.at[0], vbuf.at[4 + zb], vsend.at[2 + k], vrecv.at[3 + zb], at.core
                ).wait_recv()
            vbuf[1] = vbuf[4] + vbuf[5] + vbuf[6] + vbuf[7]
            exchange(0, at.core).start()

        def core_vectors():
            exchange(0, at.core).wait()
            vbuf[2] = vbuf[1] + vbuf[8]
            exchange(1, at.x).start()

        def x_vectors():
            exchange(1, at.x).wait()
            vbuf[3] = vbuf[2] + vbuf[9]
            exchange(2, at.y).start()

        turns = (3 - chip, flip(chip, 1), flip(chip, 2), chip)
        schedule = [
            ((1, 2), do(cross, 3)),
            ((1, 2), do(cross, 1)),
            ((2, 2), do(reduce.corner, 3)),
            ((2, 2), do(cross, 2)),
            ((3, 2), do(cross, 0)),
            ((4, 1), do(reduce.plane, 3)),
            ((5, 0), do(reduce.corner, 2)),
            ((6, 0), do(reduce.corner, 1)),
            ((6, 0), do(reduce.along, 3)),
            ((7, 0), do(reduce.plane, 2)),
            ((8, 0), spread_vectors),
            ((8, 0), do(reduce.plane, 1)),
            ((8, 0), do(reduce.corner, 0)),
            ((8, 1), do(reduce.along, 2)),
            ((8, 2), line_vectors),
            ((9, 1), core_vectors),
            ((9, 1), do(reduce.along, 1)),
            ((9, 1), do(reduce.plane, 0)),
            ((9, 2), x_vectors),
        ]
    else:
        turns = (0, 1, 2, 3)
    turn = turns[3]
    for k in (2, 1, 0):
        turn = jnp.where(step == k, turns[k], turn)

    def columns(k):
        lanes = pl.ds(pl.multiple_of(turns[k] * d, 128), d) if links else pl.ds(k * d, d)
        return pltpu.make_async_copy(dp_ref.at[:, :, lanes], dp_s.at[turns[k]], load.at[k])

    acts = [
        pltpu.make_async_copy(normed_ref, act_s.at[0], load.at[4]),
        pltpu.make_async_copy(mixed_ref, act_s.at[1], load.at[5]),
    ]
    later = [
        pltpu.make_async_copy(watt_ref.at[: 3 * d], watt_s, load.at[6]),
        pltpu.make_async_copy(resg_ref, resg_s, load.at[7]),
        pltpu.make_async_copy(kept_ref, kept_s, load.at[8]),
        pltpu.make_async_copy(result_ref, result_s, load.at[9]),
    ]

    def crop_copies(crop, size):
        span = pl.ds(LG * crop, size)
        slot = lax.rem(crop, 2)
        here = pl.ds(0, size)
        return [
            pltpu.make_async_copy(cot_ref.at[span], cot_s.at[slot, here], fetch.at[0, slot]),
            pltpu.make_async_copy(tok_ref.at[span], tok_s.at[slot, here], fetch.at[1, slot]),
            pltpu.make_async_copy(ing_s.at[slot, here], ing_ref.at[span], store.at[0, slot]),
            pltpu.make_async_copy(out_s.at[slot, here], out_ref.at[span], store.at[1, slot]),
        ]

    def place(crop, local):
        hot, span, lo, n, count = one_hot(col_s, crop, images, local)
        size = count // images
        window = lambda ref: jnp.concatenate([ref[i, pl.ds(lo, n), :] for i in range(images)], axis=0)
        taken = tn(hot, jnp.ones((images * n, 128), bf16))[:, 0:1] > 0.5
        get_cot, get_tok, put_ing, put_out = crop_copies(crop, size)
        slot = lax.rem(crop, 2)
        get_tok.wait()
        old = tok_s[slot, 0:size].reshape(count, d).astype(f32)
        new = jnp.where(taken, tn(hot, window(result_s)), old).astype(bf16)
        out_s[slot, 0:size] = new.reshape(size, images, d)
        put_out.start()
        pump(schedule, step, 1)
        get_cot.wait()
        spread = tn(hot, window(high_ref)) + tn(hot, window(low_ref))
        old = cot_s[slot, 0:size].reshape(count, d).astype(f32)
        ing_s[slot, 0:size] = jnp.where(taken, spread, old).reshape(size, images, d)
        put_ing.start()

    @pl.when(step == 0)
    def _():
        columns(0).start()
        for copy in acts:
            copy.start()
        for k in (1, 2, 3):
            columns(k).start()
        for copy in later:
            copy.start()
        vecg_s[...] = jnp.zeros_like(vecg_s)
        if links:
            at.barrier()
        for copy in acts:
            copy.wait()

    for k in range(4):
        @pl.when(step == k)
        def _(k=k):
            columns(k).wait()

    @pl.when(step < 4)
    def _():
        which = jnp.where(turn == 3, 1, 0)
        where = pl.ds(pl.multiple_of(turn * d, 128), d)
        left = dp_s[turn].reshape(total, d)
        gatt_s[where, :] = tn(left, act_s[which].reshape(total, d)).astype(bf16)

    @pl.when(step == 4)
    def _():
        for copy in later:
            copy.wait()

    pump(schedule, step, 0)

    @pl.when((step > 3) & (step < 4 + images))
    def _():
        image = step - 4
        standard, inverse = normalize(kept_s[image].astype(f32))
        ng = rg_ref[image] * vec_ref[2:3]
        for j in range(3):
            ng += nn(dp_s[j, image], watt_s[j * d : (j + 1) * d, :])
        pump(schedule, step, 1)
        grad = resg_s[image] + norm_backward(ng, standard, inverse, vec_ref[0:1])
        high = grad.astype(bf16)
        high_ref[image] = high
        low_ref[image] = (grad - high.astype(f32)).astype(bf16)
        vecg_s[0:1] += colsum(ng * standard)
        vecg_s[1:2] += colsum(ng)

    first_crop = 4 + images

    @pl.when(step == 4)
    def _():
        token_columns(idx_ref, idx_s, col_s)
        for crop in range(2):
            for copy in crop_copies(crop, LG)[:2]:
                copy.start()

    @pl.when((step == first_crop) | (step == first_crop + 1))
    def _():
        place(step - first_crop, False)

    @pl.when(step == first_crop + 1)
    def _():
        for copy in crop_copies(2, 4 * LL)[:2]:
            copy.start()
        for copy in crop_copies(0, LG)[2:]:
            copy.wait()

    @pl.when(step == first_crop + 2)
    def _():
        place(2, True)

    pump(schedule, step, 2)

    @pl.when(step == last)
    def _():
        for copy in crop_copies(1, LG)[2:] + crop_copies(2, 4 * LL)[2:]:
            copy.wait()

    if links:
        @pl.when(step == last)
        def _():
            exchange(2, at.y).wait()
            full_sum = vbuf[3] + vbuf[10]
            vecout_ref[...] = full_sum[: vecout_ref.shape[0]]
            reduce.gathered(0, *reduce.lines(), target=gout_ref)
            for make in lines:
                make().wait_send()
            reduce.sends.finish()


def adamw(grad, first, second, master, average, rate, decay):
    first_new = 0.5 * first + 0.5 * grad
    second_new = 0.5 * second + 0.5 * grad * grad
    update = first_new / (jnp.sqrt(second_new) + 1e-08)
    master_new = master - rate * (update + decay * master)
    average_new = 0.9 * average + 0.1 * master_new
    return (first_new, second_new, master_new, average_new)


GROUPS = ((0.02, 0.05), (0.02, 0.05), (0.2, 0.0))


def final_kernel(*refs):
    groups_in, rest = refs[2:17], refs[19:]
    (ing_in, out_in), (ing_ref, out_ref) = refs[:2], refs[17:19]
    qb_ref, groups_out, rest = rest[0], rest[1:18], rest[18:]
    state_s, load, fresh, store, pass_on = rest[:15], rest[15], rest[16:30], rest[30], rest[31]
    bounce = rest[32:34]
    state = [
        pltpu.make_async_copy(src, dst, load.at[i])
        for i, (src, dst) in enumerate(zip(groups_in, state_s))
    ]
    for c in state:
        c.start()
    stores, passing = [], []
    for k, (a, b) in enumerate(CROPS):
        for j, (src, dst) in enumerate(((ing_in, ing_ref), (out_in, out_ref))):
            through = bounce[j].at[a:b]
            taken = pltpu.make_async_copy(src.at[a:b], through, pass_on.at[0, j, k])
            taken.start()
            given = pltpu.make_async_copy(through, dst.at[a:b], pass_on.at[1, j, k])
            passing.append((taken, given))
    for g in range(3):
        for taken, given in passing[2 * g : 2 * g + 2]:
            taken.wait()
            given.start()
            stores.append(given)
        for c in state[5 * g : 5 * g + 5]:
            c.wait()
        grad, first, second, master, average = [ref[...] for ref in state_s[5 * g : 5 * g + 5]]
        new = adamw(grad, first, second, master, average, *GROUPS[g])
        if g < 2:
            new = new + (new[2].astype(bf16),)
        base = 5 * g
        for i, value in enumerate(new):
            fresh[base + i][...] = value
        pairs = [(fresh[base + i], base + i) for i in range(len(new))] + [(state_s[5 * g], 14 + g)]
        for src, i in pairs:
            stores.append(pltpu.make_async_copy(src, groups_out[i], store.at[i]))
            stores[-1].start()
    qb_ref[...] = state_s[10][3]
    for c in stores:
        c.wait()


def sds(*shape_dtype):
    return jax.ShapeDtypeStruct(shape_dtype[:-1], shape_dtype[-1])


def scratch(*shape_dtype):
    return pltpu.VMEM(shape_dtype[:-1], shape_dtype[-1])


def dma(*shape):
    return pltpu.SemaphoreType.DMA(shape)


def per_device(
    tokens, cotangent, kept_index,
    attention_weights, attention_first, attention_second, attention_average,
    feedforward_weights, feedforward_first, feedforward_second, feedforward_average,
    vector_weights, vector_first, vector_second, vector_average,
):
    images, length, d = tokens.shape
    ndp, nmp = lax.axis_size("dp"), lax.axis_size("mp")
    links = (ndp, nmp) == (8, MP)
    vec = vector_weights
    rows, hb = feedforward_weights.shape[1:]
    hidden = nmp * hb
    mask = masks()
    mask_specs = [full(m.shape) for m in mask]
    tok, cot = tokens.transpose(1, 0, 2), cotangent.transpose(1, 0, 2)
    comm = (lambda i: dict(collective_id=i, has_side_effects=True)) if links else (lambda i: {})

    att, ff = attention_weights.T, feedforward_weights
    if not links:
        att, ff = att.astype(bf16), ff.astype(bf16)
        att = lax.all_gather(att, ("dp", "mp"), axis=0, tiled=True)
        wff = lax.all_gather(lax.all_gather(ff, "dp", axis=1, tiled=True), "mp", axis=0)
    now = lambda *s: pl.BlockSpec((1,) + s, lambda i: (jnp.maximum(i - 1, 0), 0, 0))
    whole = lambda *s: pl.BlockSpec(s, lambda j: (0,) * len(s), pipeline_mode=pl.Buffered(1))
    rowspec = (images, RI, d)
    outs = pl.pallas_call(
        functools.partial(forward_kernel, links),
        grid=(1 + images,),
        in_specs=[ANY, ANY, full(kept_index.shape), full(vec.shape), *mask_specs]
        + ([full(att.shape), full(ff.shape)] if links else [ANY, ANY]),
        out_specs=[full(rowspec)] * 3 + [
            now(RI, 3 * d), now(RI, d), now(RI, d), now(RI, d), now(RI, d), ANY,
        ] + [ANY] * links,
        out_shape=[sds(*rowspec, bf16)] * 3 + [
            sds(images, RI, 3 * d, bf16), sds(*rowspec, bf16), sds(*rowspec, f32),
            sds(*rowspec, f32), sds(*rowspec, bf16), sds(4 * d, d, bf16),
        ] + [sds(nmp, 2, d, hb, bf16)] * links,
        scratch_shapes=[
            scratch(4 * d, d, bf16), scratch(length, images, d, bf16), scratch(length, images, d, bf16),
            scratch(8, 384, f32), scratch(384, 8, f32), dma(3),
        ] + (
            [scratch(rows, d, bf16), scratch(2, rows, hb, bf16)]
            + [dma(4, Gather.SLOTS), dma(4, Gather.SLOTS), dma(4, 1)] if links else []
        ),
        compiler_params=params(**comm(0)),
        name="forward",
    )(tok, cot, kept_index, vec, *mask, att, ff)
    kept, normed, cotk, proj, mixed, branch, resid, n2, watt = outs[:9]
    if links:
        wff = outs[9]

    outs = pl.pallas_call(
        functools.partial(feed_kernel, links),
        grid=(nmp,),
        in_specs=[
            whole(*rowspec), whole(*rowspec), ANY, ANY, full(vec.shape),
        ],
        out_specs=[full(rowspec), full(rowspec), ANY, full((nmp, hb))]
        + [full((2, 2, rows, hb))] * links,
        out_shape=[
            sds(*rowspec, bf16), sds(*rowspec, f32),
            sds(nmp, 2, d, hb, bf16), sds(nmp, hb, f32),
        ] + [sds(2, 2, rows, hb, bf16)] * links,
        scratch_shapes=[
            scratch(*rowspec, f32), scratch(images * RI, hb, bf16), scratch(images * RI, hb, bf16),
            *[scratch(RI, hb, f32)] * 4,
            scratch(nmp, 2, d, hb, bf16), scratch(2, 2, d, hb, bf16), dma(nmp + 1), dma(2),
        ] + (
            [dma(Gather.SLOTS), dma(Gather.SLOTS), dma(4)]
            + [scratch(n, 2, rows, hb, bf16) for n in (8, 8, 2, 2, 2)]
            + [dma(Reduce.SLOTS), dma(Reduce.SLOTS), dma(8)] if links else []
        ),
        compiler_params=params(**comm(3)),
        name="feedforward",
    )(n2, cotk, resid, wff, vec)
    result, n2g, gff, bg = outs[:4]

    spans = (16, 16, 4, 4, 4, 4)
    outs = pl.pallas_call(
        functools.partial(backward_kernel, links),
        grid=(images,),
        in_specs=[
            per_image(RI, d), per_image(RI, d), per_image(RI, d), per_image(RI, d),
            per_image(RI, d), per_image(RI, 3 * d),
            pl.BlockSpec((d, d), lambda i: (3, 0)), full(vec.shape), *mask_specs,
        ] + [ANY, full((2, 2, rows, hb))] * links,
        out_specs=[per_image(RI, 4 * d), per_image(RI, d), per_image(RI, 1), full((8, d))]
        + [full((2, rows, hb))] * links,
        out_shape=[
            sds(images, RI, 4 * d, bf16), sds(*rowspec, f32), sds(images, RI, 1, f32), sds(8, d, f32),
        ] + [sds(2, rows, hb, f32)] * links,
        scratch_shapes=[scratch(RI, d, bf16)] + (
            [scratch(n, 2, rows, hb, bf16) for n in (8, 8, 2, 2, 2, 4)]
            + [dma(Reduce.SLOTS), dma(Reduce.SLOTS), dma(8)] if links else []
        ),
        compiler_params=params(**comm(1)),
        name="attention_backward",
    )(n2g, cotk, branch, resid, normed, proj, watt, vec, *mask, *([gff, outs[4]] if links else []))
    dp, resg, rg, vecg = outs[:4]
    if links:
        feedforward_gradient = outs[4]

    full_d = (4 * d, d)
    outs = pl.pallas_call(
        functools.partial(grads_kernel, links),
        grid=(4 + images + 3,),
        in_specs=[ANY, ANY, ANY, full((images, RI, 1)), ANY, ANY, full(vec.shape), ANY]
        + [full(kept_index.shape), ANY, ANY, ANY]
        + [full((8, d)), full((hidden // d, d))] * links,
        out_specs=[ANY, ANY]
        + ([full((rows, d)), full(vec.shape)] if links else [full(full_d), full((8, d))]),
        out_shape=[sds(length, images, d, f32), sds(length, images, d, bf16)]
        + ([sds(rows, d, f32), sds(*vec.shape, f32)] if links else [sds(*full_d, bf16), sds(8, d, f32)]),
        scratch_shapes=([scratch(*full_d, bf16), scratch(8, d, f32)] if links else []) + [
            scratch(3 * d, d, bf16), scratch(4, *rowspec, bf16), scratch(2, *rowspec, bf16),
            scratch(*rowspec, f32), scratch(*rowspec, bf16), dma(10),
            *[scratch(*rowspec, bf16)] * 3,
            scratch(8, 384, f32), scratch(384, 8, f32),
            scratch(2, LG, images, d, bf16), scratch(2, LG, images, d, bf16),
            scratch(2, LG, images, d, f32), scratch(2, LG, images, d, bf16), dma(2, 2), dma(2, 2),
        ] + (
            [scratch(n, rows, d, bf16) for n in spans[1:]]
            + [dma(Reduce.SLOTS), dma(Reduce.SLOTS), scratch(11, 16, d, f32), dma(8), dma(8)]
            if links else []
        ),
        compiler_params=params(60, **comm(2)),
        name="attention_grads",
    )(
        dp, normed, mixed, rg, resg, kept, vec, watt, kept_index, tok, cot, result,
        *([vecg, bg] if links else []),
    )
    ing, out = outs[:2]
    if links:
        gatt, vector_gradient = outs[2:]
    else:
        gatt, vecg_in = outs[2:]
        local = jnp.concatenate([vecg_in[:2], vecg[:7], bg], axis=0)
        gatt = lax.psum_scatter(gatt, ("dp", "mp"), scatter_dimension=0, tiled=True).astype(f32)
        gff = lax.psum_scatter(gff, "mp", scatter_dimension=0, tiled=False)
        gff = lax.psum_scatter(gff, "dp", scatter_dimension=1, tiled=True)
        feedforward_gradient, vector_gradient = gff.astype(f32), lax.psum(local, ("dp", "mp"))

    state = []
    for grad, *rest in (
        (gatt, attention_first.T, attention_second.T, attention_weights.T, attention_average.T),
        (
            feedforward_gradient, feedforward_first, feedforward_second, feedforward_weights,
            feedforward_average,
        ),
        (vector_gradient, vector_first, vector_second, vector_weights, vector_average),
    ):
        state += [grad, *rest]
    fresh = []
    for g in range(3):
        fresh += [(state[5 * g].shape, f32)] * 4 + [(state[5 * g].shape, bf16)] * (g < 2)
    ing, out, qb, *new = pl.pallas_call(
        final_kernel,
        in_specs=[ANY] * 17,
        out_specs=[ANY, ANY, pl.BlockSpec(memory_space=pltpu.VMEM)] + [ANY] * (len(fresh) + 3),
        out_shape=[sds(length, images, d, f32), sds(length, images, d, bf16), sds(d, f32)]
        + [jax.ShapeDtypeStruct(*f) for f in fresh]
        + [sds(*state[5 * g].shape, f32) for g in range(3)],
        scratch_shapes=[
            *[pltpu.VMEM(v.shape, f32) for v in state], dma(15),
            *[pltpu.VMEM(*f) for f in fresh], dma(len(fresh) + 3), dma(2, 2, 3),
            scratch(length, images, d, f32), scratch(length, images, d, bf16),
        ],
        compiler_params=params(),
        name="finish",
    )(ing, out, *state)
    att_new, ff_new, vec_new = [v.T for v in new[:5]], new[5:10], new[10:14]
    gatt, feedforward_gradient, vector_gradient = new[14:]
    return (
        out.transpose(1, 0, 2), ing.transpose(1, 0, 2),
        gatt.T, *att_new, feedforward_gradient, *ff_new, vector_gradient, *vec_new, qb,
    )


def solution(mesh):
    rows = P(("dp", "mp"), None, None)
    att = P(None, ("dp", "mp"))
    feed = P(None, "dp", "mp")
    in_specs = (rows, rows, P(("dp", "mp"), None)) + (att,) * 4 + (feed,) * 4 + (P(),) * 4
    out_specs = (rows, rows) + (att,) * 6 + (feed,) * 6 + (P(),) * 6
    return jax.shard_map(
        per_device, mesh=mesh, in_specs=in_specs, out_specs=out_specs, check_vma=False
    )
```

profile of v0, /device:TPU:0, one launch (start us, length us, event | category | flops | bytes accessed | tf_op | source)
XLA Modules:
  0.0 226.8 jit_solution(10316865022726857842)
XLA Ops:
  0.7 70.9 %forward.1 = (bf16[4,272,768]{2,1,0:T(8,128)(2,1)}, bf16[4,272,768]{2,1,0:T(8,128)(2,1)}, bf16[4,272,768]{2,1,0:T(8,128)(2,1)}, bf16[4,272,2304]{2,1,0:T(8,128)(...) custom-call(bf16[542,4,768]{2,1,0:T(4,128)(2,1)} %bitcast.14, ...), custom_call_target="tpu_custom_call" | custom-call | tf_op jit(solution)/shard_map/forward/pallas_call | solution.py:1180
  71.5 60.0 %feedforward.1 = (bf16[4,272,768]{2,1,0:T(8,128)(2,1)}, f32[4,272,768]{2,1,0:T(8,128)}, bf16[4,2,768,768]{3,2,1,0:T(8,128)(2,1)}, f32[4,768]{1,0:T(4,128)}, bf16[2,2,96,768]{3,2,1,0:T(8,128)(2,1)}) custom-call(bf16[4,272,768]{2,1,0:T(8,128)(2,1)} %get-tuple-element.64.n2_ref, bf16[4,272,768]{2,1,0:T(8,128)(2,1)} %get-tuple-element.65.cot_ref.cotk_ref, ...), custom_call_target="tpu_custom_call" | custom-call | tf_op jit(solution)/shard_map/feedforward/pallas_call | solution.py:1206
  131.5 41.3 %attention_backward.1 = (bf16[4,272,3072]{2,1,0:T(8,128)(2,1)}, f32[4,272,768]{2,1,0:T(8,128)}, f32[4,272,1]{2,1,0:T(8,128)}, f32[8,768]{1,0:T(8,128)}, f32[2,96,768]{2,1,0:T(8,128)}) custom-call(f32[4,272,768]{2,1,0:T(8,128)} %get-tuple-element.68.n2g_ref, bf16[4,272,768]{2,1,0:T(8,128)(2,1)} %get-tuple-element.65.cot_ref.cotk_ref, ...), custom_call_target="tpu_custom_call" | custom-call | tf_op jit(solution)/shard_map/attention_backward/pallas_call | solution.py:1233
  172.8 43.5 %attention_grads.1 = (f32[542,4,768]{2,1,0:T(4,128)}, bf16[542,4,768]{2,1,0:T(4,128)(2,1)}, f32[96,768]{1,0:T(8,128)}, f32[13,768]{1,0:T(8,128)}) custom-call(bf16[4,272,3072]{2,1,0:T(8,128)(2,1)} %get-tuple-element.75.dp_ref, bf16[4,272,768]{2,1,0:T(8,128)(2,1)} %get-tuple-element.70.normed_ref, bf16[4,272,768]{2,1,0:T(8,128)(2,1)} %get-tuple-element.76.mixed_ref, ...), custom_call_target="tpu_custom_call" | custom-call | tf_op jit(solution)/shard_map/attention_grads/pallas_call | solution.py:1258
  216.4 10.2 %finish.1 = (f32[542,4,768]{2,1,0:T(4,128)}, bf16[542,4,768]{2,1,0:T(4,128)(2,1)}, f32[768]{0:T(1024)}, f32[96,768]{1,0:T(8,128)}, f32[96,768]{1,0:T(8,128)}, /*...) custom-call(f32[542,4,768]{2,1,0:T(4,128)} %get-tuple-element.83.ref, ...), custom_call_target="tpu_custom_call" | custom-call | tf_op jit(solution)/shard_map/finish/pallas_call | solution.py:1310
where the time goes:
time: 227 us
  Pallas kernels  226 us (100%)
    pallas_call x1, Pallas kernels, per_device(): pl.pallas_call(functools.partial(forward_kernel, links), grid=(1 + images...  70.9 us
    pallas_call x1, Pallas kernels, per_device(): pl.pallas_call(functools.partial(feed_kernel, links), grid=(nmp,), in_spe...  60 us
    pallas_call x1, Pallas kernels, per_device(): pl.pallas_call(functools.partial(grads_kernel, links), grid=(4 + images +...  43.5 us
    pallas_call x1, Pallas kernels, per_device(): pl.pallas_call(functools.partial(backward_kernel, links), grid=(images,),...  41.3 us
    pallas_call x1, Pallas kernels, per_device(): pl.pallas_call(final_kernel, in_specs=[ANY] * 17, out_specs=[ANY, ANY, pl...  10.2 us

commit v1 on v0

--- a/solution.py
+++ b/solution.py
@@ -410,20 +410,72 @@
 def forward_kernel(
     links, tok_ref, cot_ref, idx_ref, vec_ref, m0_ref, m1_ref, m2_ref, v0_ref, v1_ref, v2_ref,
     att_ref, ff_ref,
-    kept_ref, normed_ref, cotk_ref, proj_ref, mixed_ref, branch_ref, resid_ref, n2_ref,
+    kept_out, normed_out, cotk_out, proj_out, mixed_ref, branch_ref, resid_ref, n2_ref,
     watt_out, *rest,
 ):
     if links:
-        wff_ref, watt_ref, tok_s, cot_s, idx_s, col_s, load, att_s, ff_s, send, recv, local = rest
-    else:
-        watt_ref, tok_s, cot_s, idx_s, col_s, load = rest
+        wff_ref, *rest = rest
+        att_s, ff_s, send, recv, local = rest[10:]
+    watt_ref, tok_s, cot_s, idx_s, col_s, load, kept_ref, normed_ref, cotk_ref, proj_ref = rest[:10]
     step = pl.program_id(0)
     images, _, d = kept_ref.shape
+    leave = [
+        pltpu.make_async_copy(src, dst, load.at[3 + i])
+        for i, (src, dst) in enumerate(
+            (
+                (kept_ref, kept_out), (normed_ref, normed_out), (cotk_ref, cotk_out),
+                (proj_ref, proj_out),
+            )
+        )
+    ]
     loads = [
         pltpu.make_async_copy(tok_ref, tok_s, load.at[0]),
         pltpu.make_async_copy(cot_ref, cot_s, load.at[1]),
     ]
-    acts, schedule = [[]] * 6, []
+    order = (0, 1, 2, 3)
+
+    def clear(dst):
+        for i in range(images):
+            for _, hi in UNITS[:2]:
+                dst[i, hi - 16 : hi] = jnp.zeros((16, d), bf16)
+
+    def pick(crop, local, src, dst):
+        hot, span, lo, n, k = one_hot(col_s, crop, images, local)
+        got = nn(hot, src[span].reshape(k, d)).astype(bf16)
+        for i in range(images):
+            part = got[i * n : (i + 1) * n]
+            head = pl.ds(lo, 16)
+            if local:
+                dst[i, head, :] = dst[i, head, :] + part[:16]
+            else:
+                old = jnp.where(crop == 0, jnp.zeros_like(part[:16]), dst[i, head, :])
+                dst[i, head, :] = old + part[:16]
+            dst[i, pl.ds(lo + 16, n - 16), :] = part[16:]
+
+    def cot_rows():
+        loads[1].wait()
+        clear(cotk_ref)
+
+        @pl.loop(0, 2)
+        def _(crop):
+            pick(crop, False, cot_s, cotk_ref)
+
+        pick(2, True, cot_s, cotk_ref)
+
+    def project(r):
+        j = order[r]
+
+        @pl.when(j < 3)
+        def _():
+            rows_j = pl.ds(pl.multiple_of(j * d, 128), d)
+            bias = jnp.where(j == 1, 0.0, jnp.where(j == 0, vec_ref[3:4], vec_ref[4:5]))
+
+            @pl.loop(0, images)
+            def _(i):
+                part = nt(normed_ref[i], watt_ref[rows_j, :]) + bias
+                proj_ref[i, :, rows_j] = part.astype(bf16)
+
+    acts, schedule = [[]] * 5 + [[cot_rows]], []
     if links:
         at = Place()
         rows = att_ref.shape[0]
@@ -446,6 +498,16 @@
             )
 
         (a0, a1), (f0, f1) = [att_half(h) for h in (0, 1)], [feed_half(h) for h in (0, 1)]
+        chip = lax.div(at.dp, 2)
+        order = (chip, flip(chip, 1), flip(chip, 2), 3 - chip)
+
+        def ready(r):
+            for part in (a0, a1):
+                for e in range(4):
+                    part.got(part.C + 4 * e + r, e, at.mates[r])
+                if r == 0:
+                    part.keep(0).wait()
+
         acts = [
             [a1.begin, a0.begin],
             [do(a1.along, 1), do(a1.plane, 0), do(a0.along, 1), do(a0.along, 2), do(a1.along, 2)],
@@ -453,10 +515,15 @@
             [do(a1.along, 3), f0.direct, do(a1.plane, 1), do(a0.plane, 2)],
             [do(a0.plane, 0)],
             [
-                do(a0.plane, 3), do(a0.plane, 1), do(a1.plane, 3), do(a1.plane, 2),
+                do(ready, 0), do(project, 0),
+                do(a0.plane, 3), do(a0.plane, 1), do(a1.plane, 3), do(a1.plane, 2), cot_rows,
+                do(ready, 1), do(project, 1),
                 do(a0.corner, 0), do(a1.corner, 1), do(a0.corner, 3), do(a1.corner, 2),
-                do(a1.corner, 0), f1.direct, do(a0.corner, 1), do(a0.corner, 2), do(a1.corner, 3),
+                do(a1.corner, 0), f1.direct,
+                do(ready, 2), do(project, 2),
+                do(a0.corner, 1), do(a0.corner, 2), do(a1.corner, 3),
                 do(f0.arrived, 2), do(f0.spread, 2),
+                do(ready, 3), do(project, 3),
             ],
         ]
         schedule = [
@@ -479,24 +546,6 @@
         fetch = pltpu.make_async_copy(att_ref, watt_ref, load.at[2])
     store = pltpu.make_async_copy(watt_ref, watt_out, load.at[2])
 
-    def clear(dst):
-        for i in range(images):
-            for _, hi in UNITS[:2]:
-                dst[i, hi - 16 : hi] = jnp.zeros((16, d), bf16)
-
-    def pick(crop, local, src, dst):
-        hot, span, lo, n, k = one_hot(col_s, crop, images, local)
-        got = nn(hot, src[span].reshape(k, d)).astype(bf16)
-        for i in range(images):
-            part = got[i * n : (i + 1) * n]
-            head = pl.ds(lo, 16)
-            if local:
-                dst[i, head, :] = dst[i, head, :] + part[:16]
-            else:
-                old = jnp.where(crop == 0, jnp.zeros_like(part[:16]), dst[i, head, :])
-                dst[i, head, :] = old + part[:16]
-            dst[i, pl.ds(lo + 16, n - 16), :] = part[16:]
-
     def run(point):
         for action in acts[point]:
             action()
@@ -531,15 +580,13 @@
             if i == 1:
                 run(4)
         run(5)
-        if links:
-            for e in range(4):
-                a0.finish(e)
-                a1.finish(e)
-            a0.keep(0).wait()
-            a1.keep(0).wait()
-        else:
+        if not links:
             fetch.wait()
+            for r in range(3):
+                project(r)
         store.start()
+        for c in leave:
+            c.start()
 
     pump(schedule, step, 0)
 
@@ -547,35 +594,16 @@
     def _():
         image = step - 1
         normed = normed_ref[image]
-        for j, row in ((0, 3), (1, None), (2, 4)):
-            part = nt(normed, watt_ref[j * d : (j + 1) * d, :])
-            if row is not None:
-                part = part + vec_ref[row : row + 1]
-            proj_ref[0, :, j * d : (j + 1) * d] = part.astype(bf16)
         pump(schedule, step, 1)
-
-        @pl.when(step == 2)
-        def _():
-            loads[1].wait()
-            clear(cotk_ref)
-
-        @pl.when((step == 2) | (step == 3))
-        def _():
-            pick(step - 2, False, cot_s, cotk_ref)
-
-        @pl.when(step == 4)
-        def _():
-            pick(2, True, cot_s, cotk_ref)
-
         mrefs, vrefs = (m0_ref, m1_ref, m2_ref), (v0_ref, v1_ref, v2_ref)
         for pair in range(PAIRS):
             cols = lambda j: slice(j * d + pair * W2L, j * d + (pair + 1) * W2L)
             tail = None
             for unit, (lo, hi) in enumerate(UNITS):
-                qs = split_heads(proj_ref[0, lo:hi, cols(0)], HD ** -0.5)
-                st = nt(proj_ref[0, lo:hi, cols(1)], qs) + mrefs[unit][...]
+                qs = split_heads(proj_ref[image, lo:hi, cols(0)], HD ** -0.5)
+                st = nt(proj_ref[image, lo:hi, cols(1)], qs) + mrefs[unit][...]
                 pt = softmax_keys(st, vrefs[unit][0:1]).astype(bf16)
-                out = join_heads(tn(pt, proj_ref[0, lo:hi, cols(2)]))
+                out = join_heads(tn(pt, proj_ref[image, lo:hi, cols(2)]))
                 tail = store_window(mixed_ref, 0, lo, hi, unit == 2, cols(0), out, tail)
             if pair == 2:
                 pump(schedule, step, 3)
@@ -596,7 +624,8 @@
                 feed.keep(0).wait()
             for part in (a0, a1, f0, f1):
                 part.sends.finish()
-        store.wait()
+        for c in [store] + leave:
+            c.wait()
 
 
 def router_score(normed, vec_ref):
@@ -658,15 +687,15 @@
 
         schedule = [
             ((1, 0), do(gather.plane, 1)),
-            ((1, 3), do(gather.plane, 0)),
-            ((1, 4), do(cross, 3)),
+            ((1, 0), do(gather.plane, 0)),
+            ((1, 0), do(cross, 3)),
             ((2, 0), do(gather.corner, 1)),
             ((2, 0), do(reduce.corner, 3)),
             ((2, 0), do(cross, 2)),
             ((2, 0), do(ready, 1)),
-            ((2, 2), do(reduce.corner, 2)),
-            ((2, 2), do(gather.corner, 0)),
-            ((2, 5), do(reduce.plane, 3)),
+            ((2, 0), do(reduce.corner, 2)),
+            ((2, 0), do(gather.corner, 0)),
+            ((3, 0), do(reduce.plane, 3)),
             ((3, 0), do(ready, 0)),
             ((3, 0), do(reduce.plane, 2)),
         ]
@@ -1182,16 +1211,15 @@
         grid=(1 + images,),
         in_specs=[ANY, ANY, full(kept_index.shape), full(vec.shape), *mask_specs]
         + ([full(att.shape), full(ff.shape)] if links else [ANY, ANY]),
-        out_specs=[full(rowspec)] * 3 + [
-            now(RI, 3 * d), now(RI, d), now(RI, d), now(RI, d), now(RI, d), ANY,
-        ] + [ANY] * links,
+        out_specs=[ANY] * 4 + [now(RI, d)] * 4 + [ANY] + [ANY] * links,
         out_shape=[sds(*rowspec, bf16)] * 3 + [
             sds(images, RI, 3 * d, bf16), sds(*rowspec, bf16), sds(*rowspec, f32),
             sds(*rowspec, f32), sds(*rowspec, bf16), sds(4 * d, d, bf16),
         ] + [sds(nmp, 2, d, hb, bf16)] * links,
         scratch_shapes=[
             scratch(4 * d, d, bf16), scratch(length, images, d, bf16), scratch(length, images, d, bf16),
-            scratch(8, 384, f32), scratch(384, 8, f32), dma(3),
+            scratch(8, 384, f32), scratch(384, 8, f32), dma(7),
+            *[scratch(*rowspec, bf16)] * 3, scratch(images, RI, 3 * d, bf16),
         ] + (
             [scratch(rows, d, bf16), scratch(2, rows, hb, bf16)]
             + [dma(4, Gather.SLOTS), dma(4, Gather.SLOTS), dma(4, 1)] if links else []

time: 227 us -> 223 us (0.982)
  Pallas kernels: 226 us -> 221 us
    pallas_call x1, Pallas kernels: 70.9 us -> 67.8 us  [per_device(): pl.pallas_call(functools.partial(forward_kernel, links), grid=(1 + images...]
    pallas_call x1, Pallas kernels: 60 us -> 57.2 us  [per_device(): pl.pallas_call(functools.partial(feed_kernel, links), grid=(nmp,), in_spe...]
where the time goes in v1:
time: 223 us; the launch traced here: 222 us
  Pallas kernels  221 us (99%)
    pallas_call x1, Pallas kernels, per_device(): pl.pallas_call(functools.partial(forward_kernel, links), grid=(1 + images...  67.8 us
    pallas_call x1, Pallas kernels, per_device(): pl.pallas_call(functools.partial(feed_kernel, links), grid=(nmp,), in_spe...  57.2 us
    pallas_call x1, Pallas kernels, per_device(): pl.pallas_call(functools.partial(grads_kernel, links), grid=(4 + images +...  44.3 us
    pallas_call x1, Pallas kernels, per_device(): pl.pallas_call(functools.partial(backward_kernel, links), grid=(images,),...  42 us
    pallas_call x1, Pallas kernels, per_device(): pl.pallas_call(final_kernel, in_specs=[ANY] * 17, out_specs=[ANY, ANY, pl...  10.2 us

profile of v1, /device:TPU:0, one launch (start us, length us, event | category | flops | bytes accessed | tf_op | source)
XLA Modules:
  0.0 222.4 jit_solution(196670979208524436)
XLA Ops:
  0.7 67.8 %forward.1 = (bf16[4,272,768]{2,1,0:T(8,128)(2,1)}, bf16[4,272,768]{2,1,0:T(8,128)(2,1)}, bf16[4,272,768]{2,1,0:T(8,128)(2,1)}, bf16[4,272,2304]{2,1,0:T(8,128)(...) custom-call(bf16[542,4,768]{2,1,0:T(4,128)(2,1)} %bitcast.14, ...), custom_call_target="tpu_custom_call" | custom-call | tf_op jit(solution)/shard_map/forward/pallas_call | solution.py:1209
  68.4 57.2 %feedforward.1 = (bf16[4,272,768]{2,1,0:T(8,128)(2,1)}, f32[4,272,768]{2,1,0:T(8,128)}, bf16[4,2,768,768]{3,2,1,0:T(8,128)(2,1)}, f32[4,768]{1,0:T(4,128)}, bf16[2,2,96,768]{3,2,1,0:T(8,128)(2,1)}) custom-call(bf16[4,272,768]{2,1,0:T(8,128)(2,1)} %get-tuple-element.64.n2_ref, bf16[4,272,768]{2,1,0:T(8,128)(2,1)} %get-tuple-element.65.cot_ref.cotk_ref, ...), custom_call_target="tpu_custom_call" | custom-call | tf_op jit(solution)/shard_map/feedforward/pallas_call | solution.py:1234
  125.6 42.0 %attention_backward.1 = (bf16[4,272,3072]{2,1,0:T(8,128)(2,1)}, f32[4,272,768]{2,1,0:T(8,128)}, f32[4,272,1]{2,1,0:T(8,128)}, f32[8,768]{1,0:T(8,128)}, f32[2,96,768]{2,1,0:T(8,128)}) custom-call(f32[4,272,768]{2,1,0:T(8,128)} %get-tuple-element.68.n2g_ref, bf16[4,272,768]{2,1,0:T(8,128)(2,1)} %get-tuple-element.65.cot_ref.cotk_ref, ...), custom_call_target="tpu_custom_call" | custom-call | tf_op jit(solution)/shard_map/attention_backward/pallas_call | solution.py:1261
  167.7 44.3 %attention_grads.1 = (f32[542,4,768]{2,1,0:T(4,128)}, bf16[542,4,768]{2,1,0:T(4,128)(2,1)}, f32[96,768]{1,0:T(8,128)}, f32[13,768]{1,0:T(8,128)}) custom-call(bf16[4,272,3072]{2,1,0:T(8,128)(2,1)} %get-tuple-element.75.dp_ref, bf16[4,272,768]{2,1,0:T(8,128)(2,1)} %get-tuple-element.70.normed_ref, bf16[4,272,768]{2,1,0:T(8,128)(2,1)} %get-tuple-element.76.mixed_ref, ...), custom_call_target="tpu_custom_call" | custom-call | tf_op jit(solution)/shard_map/attention_grads/pallas_call | solution.py:1286
  212.0 10.2 %finish.1 = (f32[542,4,768]{2,1,0:T(4,128)}, bf16[542,4,768]{2,1,0:T(4,128)(2,1)}, f32[768]{0:T(1024)}, f32[96,768]{1,0:T(8,128)}, f32[96,768]{1,0:T(8,128)}, /*...) custom-call(f32[542,4,768]{2,1,0:T(4,128)} %get-tuple-element.83.ref, ...), custom_call_target="tpu_custom_call" | custom-call | tf_op jit(solution)/shard_map/finish/pallas_call | solution.py:1338

commit v2 on v1

--- a/solution.py
+++ b/solution.py
@@ -512,35 +512,33 @@
             [a1.begin, a0.begin],
             [do(a1.along, 1), do(a1.plane, 0), do(a0.along, 1), do(a0.along, 2), do(a1.along, 2)],
             [do(a0.along, 3)],
-            [do(a1.along, 3), f0.direct, do(a1.plane, 1), do(a0.plane, 2)],
+            [do(a1.along, 3), f0.direct, f1.direct, do(a1.plane, 1), do(a0.plane, 2)],
             [do(a0.plane, 0)],
             [
                 do(ready, 0), do(project, 0),
                 do(a0.plane, 3), do(a0.plane, 1), do(a1.plane, 3), do(a1.plane, 2), cot_rows,
                 do(ready, 1), do(project, 1),
                 do(a0.corner, 0), do(a1.corner, 1), do(a0.corner, 3), do(a1.corner, 2),
-                do(a1.corner, 0), f1.direct,
+                do(a1.corner, 0),
                 do(ready, 2), do(project, 2),
                 do(a0.corner, 1), do(a0.corner, 2), do(a1.corner, 3),
-                do(f0.arrived, 2), do(f0.spread, 2),
+                do(f0.arrived, 2), do(f0.spread, 2), do(f0.arrived, 3), do(f0.spread, 3),
                 do(ready, 3), do(project, 3),
             ],
         ]
         schedule = [
-            ((1, 3), do(f0.arrived, 3)),
-            ((1, 3), do(f0.spread, 3)),
-            ((2, 1), do(f1.arrived, 2)),
-            ((2, 1), do(f1.spread, 2)),
-            ((3, 0), do(f1.arrived, 3)),
-            ((3, 0), do(f1.spread, 3)),
-            ((3, 0), do(f0.plane, 2)),
-            ((3, 1), do(f1.plane, 2)),
-            ((3, 1), do(f0.plane, 3)),
-            ((3, 3), do(f1.plane, 3)),
+            ((1, 3), do(f1.arrived, 2)),
+            ((1, 3), do(f1.spread, 2)),
+            ((1, 3), do(f1.arrived, 3)),
+            ((1, 3), do(f1.spread, 3)),
+            ((2, 3), do(f0.plane, 2)),
+            ((2, 3), do(f0.plane, 3)),
+            ((3, 3), do(f1.plane, 2)),
+            ((4, 1), do(f1.plane, 3)),
+            ((4, 1), do(f0.corner, 2)),
+            ((4, 1), do(f0.corner, 3)),
+            ((4, 3), do(f1.corner, 2)),
             ((4, 3), do(f1.corner, 3)),
-            ((4, 3), do(f0.corner, 3)),
-            ((4, 3), do(f1.corner, 2)),
-            ((4, 3), do(f0.corner, 2)),
         ]
     else:
         fetch = pltpu.make_async_copy(att_ref, watt_ref, load.at[2])
@@ -635,13 +633,12 @@
 
 def feed_kernel(
     links, n2_ref, cot_ref, resid_ref, w_ref, vec_ref,
-    result_ref, n2g_ref, gff_ref, bg_ref, *rest,
+    result_out, n2g_out, gff_ref, bg_ref, *rest,
 ):
     if links:
-        acc_ref, out_s, act_s, ig_s, i0, i1, a0, a1, w_s, g_s, load, store = rest[:12]
-        send, recv, local, a, c, dd, x, y, rsend, rrecv, rlocal = rest[12:]
-    else:
-        out_s, act_s, ig_s, i0, i1, a0, a1, w_s, g_s, load, store = rest
+        acc_ref, *rest = rest
+        send, recv, local, a, c, dd, x, y, rsend, rrecv, rlocal = rest[13:]
+    result_ref, n2g_ref, out_s, act_s, ig_s, i0, i1, a0, a1, w_s, g_s, load, store = rest[:13]
     inner_s, ag_s = (i0, i1), (a0, a1)
     step = pl.program_id(0)
     last = pl.num_programs(0) - 1
@@ -760,7 +757,17 @@
             first(i + 1)
         second(i)
 
-    pump(schedule, step, 5)
+    leave = [
+        pltpu.make_async_copy(n2g_ref, n2g_out, store.at[2]),
+        pltpu.make_async_copy(result_ref, result_out, store.at[3]),
+    ]
+
+    @pl.when(step == last)
+    def _():
+        leave[0].start()
+        result_ref[...] = (out_s[...] + vec_ref[8:9]).astype(bf16)
+        leave[1].start()
+
     n2 = n2_ref[...].reshape(images * RI, d)
     cot = cot_ref[...].reshape(images * RI, d)
     g_s[slot, 0] = tn(n2, ig_s[...]).astype(bf16)
@@ -769,7 +776,8 @@
 
     @pl.when(step == last)
     def _():
-        result_ref[...] = (out_s[...] + vec_ref[8:9]).astype(bf16)
+        for c in leave:
+            c.wait()
         if links:
             reduce.gathered(3, target=acc_ref.at[0])
             reduce.gathered(2, target=acc_ref.at[1])
@@ -812,9 +820,9 @@
         schedule = [
             ((0, 0), start),
             ((0, 1), do(reduce.corner, 1)),
-            ((0, 3), do(reduce.send_along, 3, lambda: acc_ref.at[0])),
+            ((0, 1), do(reduce.send_along, 3, lambda: acc_ref.at[0])),
             ((1, 1), do(reduce.plane, 1)),
-            ((1, 3), do(reduce.corner, 0)),
+            ((2, 0), do(reduce.corner, 0)),
             ((2, 1), do(reduce.along, 1)),
             ((3, 0), do(reduce.plane, 0)),
         ]
@@ -1237,16 +1245,17 @@
         in_specs=[
             whole(*rowspec), whole(*rowspec), ANY, ANY, full(vec.shape),
         ],
-        out_specs=[full(rowspec), full(rowspec), ANY, full((nmp, hb))]
+        out_specs=[ANY, ANY, ANY, full((nmp, hb))]
         + [full((2, 2, rows, hb))] * links,
         out_shape=[
             sds(*rowspec, bf16), sds(*rowspec, f32),
             sds(nmp, 2, d, hb, bf16), sds(nmp, hb, f32),
         ] + [sds(2, 2, rows, hb, bf16)] * links,
         scratch_shapes=[
+            scratch(*rowspec, bf16), scratch(*rowspec, f32),
             scratch(*rowspec, f32), scratch(images * RI, hb, bf16), scratch(images * RI, hb, bf16),
             *[scratch(RI, hb, f32)] * 4,
-            scratch(nmp, 2, d, hb, bf16), scratch(2, 2, d, hb, bf16), dma(nmp + 1), dma(2),
+            scratch(nmp, 2, d, hb, bf16), scratch(2, 2, d, hb, bf16), dma(nmp + 1), dma(4),
         ] + (
             [dma(Gather.SLOTS), dma(Gather.SLOTS), dma(4)]
             + [scratch(n, 2, rows, hb, bf16) for n in (8, 8, 2, 2, 2)]

time: 223 us -> 221 us (level)
    pallas_call x1, Pallas kernels: 57.2 us -> 54.2 us  [per_device(): pl.pallas_call(functools.partial(feed_kernel, links), grid=(nmp,), in_spe...]
where the time goes in v2:
time: 221 us
  Pallas kernels  220 us (100%)
    pallas_call x1, Pallas kernels, per_device(): pl.pallas_call(functools.partial(forward_kernel, links), grid=(1 + images...  69.1 us
    pallas_call x1, Pallas kernels, per_device(): pl.pallas_call(functools.partial(feed_kernel, links), grid=(nmp,), in_spe...  54.2 us
    pallas_call x1, Pallas kernels, per_device(): pl.pallas_call(functools.partial(grads_kernel, links), grid=(4 + images +...  43.6 us
    pallas_call x1, Pallas kernels, per_device(): pl.pallas_call(functools.partial(backward_kernel, links), grid=(images,),...  42.6 us
    pallas_call x1, Pallas kernels, per_device(): pl.pallas_call(final_kernel, in_specs=[ANY] * 17, out_specs=[ANY, ANY, pl...  10.2 us

profile of v2, /device:TPU:0, one launch (start us, length us, event | category | flops | bytes accessed | tf_op | source)
XLA Modules:
  0.0 220.6 jit_solution(4560003489273874953)
XLA Ops:
  0.7 69.1 %forward.1 = (bf16[4,272,768]{2,1,0:T(8,128)(2,1)}, bf16[4,272,768]{2,1,0:T(8,128)(2,1)}, bf16[4,272,768]{2,1,0:T(8,128)(2,1)}, bf16[4,272,2304]{2,1,0:T(8,128)(...) custom-call(bf16[542,4,768]{2,1,0:T(4,128)(2,1)} %bitcast.14, ...), custom_call_target="tpu_custom_call" | custom-call | tf_op jit(solution)/shard_map/forward/pallas_call | solution.py:1217
  69.8 54.2 %feedforward.1 = (bf16[4,272,768]{2,1,0:T(8,128)(2,1)}, f32[4,272,768]{2,1,0:T(8,128)}, bf16[4,2,768,768]{3,2,1,0:T(8,128)(2,1)}, f32[4,768]{1,0:T(4,128)}, bf16[2,2,96,768]{3,2,1,0:T(8,128)(2,1)}) custom-call(bf16[4,272,768]{2,1,0:T(8,128)(2,1)} %get-tuple-element.64.n2_ref, bf16[4,272,768]{2,1,0:T(8,128)(2,1)} %get-tuple-element.65.cot_ref.cotk_ref, ...), custom_call_target="tpu_custom_call" | custom-call | tf_op jit(solution)/shard_map/feedforward/pallas_call | solution.py:1242
  124.0 42.6 %attention_backward.1 = (bf16[4,272,3072]{2,1,0:T(8,128)(2,1)}, f32[4,272,768]{2,1,0:T(8,128)}, f32[4,272,1]{2,1,0:T(8,128)}, f32[8,768]{1,0:T(8,128)}, f32[2,96,768]{2,1,0:T(8,128)}) custom-call(f32[4,272,768]{2,1,0:T(8,128)} %get-tuple-element.68.n2g_ref, bf16[4,272,768]{2,1,0:T(8,128)(2,1)} %get-tuple-element.65.cot_ref.cotk_ref, ...), custom_call_target="tpu_custom_call" | custom-call | tf_op jit(solution)/shard_map/attention_backward/pallas_call | solution.py:1270
  166.6 43.6 %attention_grads.1 = (f32[542,4,768]{2,1,0:T(4,128)}, bf16[542,4,768]{2,1,0:T(4,128)(2,1)}, f32[96,768]{1,0:T(8,128)}, f32[13,768]{1,0:T(8,128)}) custom-call(bf16[4,272,3072]{2,1,0:T(8,128)(2,1)} %get-tuple-element.75.dp_ref, bf16[4,272,768]{2,1,0:T(8,128)(2,1)} %get-tuple-element.70.normed_ref, bf16[4,272,768]{2,1,0:T(8,128)(2,1)} %get-tuple-element.76.mixed_ref, ...), custom_call_target="tpu_custom_call" | custom-call | tf_op jit(solution)/shard_map/attention_grads/pallas_call | solution.py:1295
  210.2 10.2 %finish.1 = (f32[542,4,768]{2,1,0:T(4,128)}, bf16[542,4,768]{2,1,0:T(4,128)(2,1)}, f32[768]{0:T(1024)}, f32[96,768]{1,0:T(8,128)}, f32[96,768]{1,0:T(8,128)}, /*...) custom-call(f32[542,4,768]{2,1,0:T(4,128)} %get-tuple-element.83.ref, ...), custom_call_target="tpu_custom_call" | custom-call | tf_op jit(solution)/shard_map/finish/pallas_call | solution.py:1347

commit v3 on v2

--- a/solution.py
+++ b/solution.py
@@ -527,14 +527,14 @@
             ],
         ]
         schedule = [
-            ((1, 3), do(f1.arrived, 2)),
-            ((1, 3), do(f1.spread, 2)),
-            ((1, 3), do(f1.arrived, 3)),
-            ((1, 3), do(f1.spread, 3)),
-            ((2, 3), do(f0.plane, 2)),
-            ((2, 3), do(f0.plane, 3)),
-            ((3, 3), do(f1.plane, 2)),
-            ((4, 1), do(f1.plane, 3)),
+            ((1, 1), do(f1.arrived, 2)),
+            ((1, 1), do(f1.spread, 2)),
+            ((1, 1), do(f1.arrived, 3)),
+            ((1, 1), do(f1.spread, 3)),
+            ((2, 1), do(f0.plane, 2)),
+            ((2, 1), do(f0.plane, 3)),
+            ((3, 1), do(f1.plane, 2)),
+            ((3, 1), do(f1.plane, 3)),
             ((4, 1), do(f0.corner, 2)),
             ((4, 1), do(f0.corner, 3)),
             ((4, 3), do(f1.corner, 2)),

time: 221 us -> 219 us (level)
  Pallas kernels: 220 us -> 217 us
    pallas_call x1, Pallas kernels: 69.1 us -> 66.7 us  [per_device(): pl.pallas_call(functools.partial(forward_kernel, links), grid=(1 + images...]
where the time goes in v3:
time: 219 us; the launch traced here: 218 us
  Pallas kernels  217 us (99%)
    pallas_call x1, Pallas kernels, per_device(): pl.pallas_call(functools.partial(forward_kernel, links), grid=(1 + images...  66.7 us
    pallas_call x1, Pallas kernels, per_device(): pl.pallas_call(functools.partial(feed_kernel, links), grid=(nmp,), in_spe...  54.6 us
    pallas_call x1, Pallas kernels, per_device(): pl.pallas_call(functools.partial(grads_kernel, links), grid=(4 + images +...  44.5 us
    pallas_call x1, Pallas kernels, per_device(): pl.pallas_call(functools.partial(backward_kernel, links), grid=(images,),...  41.3 us
    pallas_call x1, Pallas kernels, per_device(): pl.pallas_call(final_kernel, in_specs=[ANY] * 17, out_specs=[ANY, ANY, pl...  10.2 us

profile of v3, /device:TPU:0, one launch (start us, length us, event | category | flops | bytes accessed | tf_op | source)
XLA Modules:
  0.0 218.3 jit_solution(9340382379301430060)
XLA Ops:
  0.7 66.7 %forward.1 = (bf16[4,272,768]{2,1,0:T(8,128)(2,1)}, bf16[4,272,768]{2,1,0:T(8,128)(2,1)}, bf16[4,272,768]{2,1,0:T(8,128)(2,1)}, bf16[4,272,2304]{2,1,0:T(8,128)(...) custom-call(bf16[542,4,768]{2,1,0:T(4,128)(2,1)} %bitcast.14, ...), custom_call_target="tpu_custom_call" | custom-call | tf_op jit(solution)/shard_map/forward/pallas_call | solution.py:1217
  67.4 54.6 %feedforward.1 = (bf16[4,272,768]{2,1,0:T(8,128)(2,1)}, f32[4,272,768]{2,1,0:T(8,128)}, bf16[4,2,768,768]{3,2,1,0:T(8,128)(2,1)}, f32[4,768]{1,0:T(4,128)}, bf16[2,2,96,768]{3,2,1,0:T(8,128)(2,1)}) custom-call(bf16[4,272,768]{2,1,0:T(8,128)(2,1)} %get-tuple-element.64.n2_ref, bf16[4,272,768]{2,1,0:T(8,128)(2,1)} %get-tuple-element.65.cot_ref.cotk_ref, ...), custom_call_target="tpu_custom_call" | custom-call | tf_op jit(solution)/shard_map/feedforward/pallas_call | solution.py:1242
  122.0 41.3 %attention_backward.1 = (bf16[4,272,3072]{2,1,0:T(8,128)(2,1)}, f32[4,272,768]{2,1,0:T(8,128)}, f32[4,272,1]{2,1,0:T(8,128)}, f32[8,768]{1,0:T(8,128)}, f32[2,96,768]{2,1,0:T(8,128)}) custom-call(f32[4,272,768]{2,1,0:T(8,128)} %get-tuple-element.68.n2g_ref, bf16[4,272,768]{2,1,0:T(8,128)(2,1)} %get-tuple-element.65.cot_ref.cotk_ref, ...), custom_call_target="tpu_custom_call" | custom-call | tf_op jit(solution)/shard_map/attention_backward/pallas_call | solution.py:1270
  163.3 44.5 %attention_grads.1 = (f32[542,4,768]{2,1,0:T(4,128)}, bf16[542,4,768]{2,1,0:T(4,128)(2,1)}, f32[96,768]{1,0:T(8,128)}, f32[13,768]{1,0:T(8,128)}) custom-call(bf16[4,272,3072]{2,1,0:T(8,128)(2,1)} %get-tuple-element.75.dp_ref, bf16[4,272,768]{2,1,0:T(8,128)(2,1)} %get-tuple-element.70.normed_ref, bf16[4,272,768]{2,1,0:T(8,128)(2,1)} %get-tuple-element.76.mixed_ref, ...), custom_call_target="tpu_custom_call" | custom-call | tf_op jit(solution)/shard_map/attention_grads/pallas_call | solution.py:1295
  207.9 10.2 %finish.1 = (f32[542,4,768]{2,1,0:T(4,128)}, bf16[542,4,768]{2,1,0:T(4,128)(2,1)}, f32[768]{0:T(1024)}, f32[96,768]{1,0:T(8,128)}, f32[96,768]{1,0:T(8,128)}, /*...) custom-call(f32[542,4,768]{2,1,0:T(4,128)} %get-tuple-element.83.ref, ...), custom_call_target="tpu_custom_call" | custom-call | tf_op jit(solution)/shard_map/finish/pallas_call | solution.py:1347
